TPU v7x, 32 devices: a whole 2x2x4 slice. The times are simulated.
32 devices in a mesh: grp: 2 (over y), pts: 8 (over z, x), rcv: 2 (over core).
Axes of the slice: x: 2, y: 2, z: 4, core: 2. Of those that a mesh axis runs over, the one named last changes fastest.
Arguments:
- src_green: float32 [2, 128, 2048], P(None, 'grp', 'pts'), parts along dimension 1, may hold values from -0.125 to 0.125
- rcv_green: float32 [2, 2048, 2048], P(None, ('grp', 'rcv'), 'pts'), parts along dimension 1, may hold values from -6 to 6
- model: float32 [4096], P(('grp', 'pts')), parts along dimension 0, may hold values from -6 to 6
- observed: float32 [128, 2, 1024], P(('grp', 'pts'), None, 'rcv'), parts along dimension 0, may hold values from -30 to 30, as said below
Outputs:
- gradient: float32 [4096], P(('grp', 'pts')), parts along dimension 0
There are 2 independent parts, one for each index of `grp`. A program takes and returns all parts, laid end to end along the dimension named above; each array names one. Nothing has to cross between parts.
Inputs may be any that keep to these rules, and one draw needn't show every extreme that they name: `observed`: complex data (real and imaginary parts) whose scale varies with the source.
All inputs are finite; a program needn't handle non-finite values.
Results may differ from a plain program's by a relative error of at most 0.000068.
Values sent between devices are 32-bit elements; how exact they have to be, the bound alone decides.
A program may use at most 64 MiB of HBM per device.

v0:
```python
import jax
import jax.numpy as jnp
from jax import lax
from jax.sharding import PartitionSpec as P


def modelled_data(scaled, rcv_green):
    highest = lax.Precision.HIGHEST
    real_part = jnp.dot(
        scaled[0], rcv_green[0].T, precision=highest, preferred_element_type=jnp.float32
    ) - jnp.dot(scaled[1], rcv_green[1].T, precision=highest, preferred_element_type=jnp.float32)
    imag_part = jnp.dot(
        scaled[0], rcv_green[1].T, precision=highest, preferred_element_type=jnp.float32
    ) + jnp.dot(scaled[1], rcv_green[0].T, precision=highest, preferred_element_type=jnp.float32)
    return jnp.stack([real_part, imag_part], axis=1)


def image_terms(weighted, rcv_green, src_rows):
    highest = lax.Precision.HIGHEST
    back_real = jnp.dot(
        weighted[:, 0, :], rcv_green[0], precision=highest, preferred_element_type=jnp.float32
    ) + jnp.dot(
        weighted[:, 1, :], rcv_green[1], precision=highest, preferred_element_type=jnp.float32
    )
    back_imag = jnp.dot(
        weighted[:, 1, :], rcv_green[0], precision=highest, preferred_element_type=jnp.float32
    ) - jnp.dot(
        weighted[:, 0, :], rcv_green[1], precision=highest, preferred_element_type=jnp.float32
    )
    return jnp.sum(src_rows[0] * back_real + src_rows[1] * back_imag, axis=0)


def cauchy_weights(resid, spread_sq):
    energy = resid[:, 0, :] ** 2 + resid[:, 1, :] ** 2
    return resid / (1.0 + energy / spread_sq)[:, None, :]


def local(src_green, rcv_green, model, observed):
    num_sources = src_green.shape[1]
    num_points = src_green.shape[2] * lax.axis_size("pts")
    num_receivers = rcv_green.shape[1] * lax.axis_size("rcv")
    scaled = src_green * model[None, None, :]
    all_observed = lax.all_gather(observed, "pts", axis=0, tiled=True)
    modelled = lax.psum(modelled_data(scaled, rcv_green), "pts")
    resid = modelled - all_observed
    energy_sum = jnp.sum(resid[:, 0, :] ** 2 + resid[:, 1, :] ** 2)
    total = lax.psum(energy_sum, "rcv")
    spread_sq = total / (num_sources * num_receivers) + 1e-06
    weighted = cauchy_weights(resid, spread_sq)
    partial_image = image_terms(weighted, rcv_green, src_green)
    image = lax.psum(partial_image, "rcv")
    return image * jnp.sqrt(jnp.float32(num_points) / (num_receivers * num_sources))


def solution(mesh):
    placed = (
        P(None, "grp", "pts"),
        P(None, ("grp", "rcv"), "pts"),
        P(("grp", "pts")),
        P(("grp", "pts"), None, "rcv"),
    )
    return jax.shard_map(
        local, mesh=mesh, in_specs=placed, out_specs=P(("grp", "pts")), check_vma=False
    )
```

profile of v0, /device:TPU:0, one launch (start us, length us, event | category | flops | bytes accessed | tf_op | source)
XLA Modules:
  0.0 104.5 jit_solution(12044138015975517374)
XLA Ops:
  6.5 0.0 copy-start
  6.5 0.0 all-reduce.2.cloned.1.call-start
  6.5 1.0 broadcast_multiply_fusion
  7.5 1.6 %fusion.16 = f32[64,512]{1,0:T(8,128)S(1)} fusion(f32[2,512,256]{2,1,0:T(8,128)} %param.5, f32[2,64,256]{2,1,0:T(8,128)S(1)} %broadcast_multiply_fusion), kind=kOutput, calls=%fused_computation.20 | convolution fusion | flops 100663296 | bytes 720896 | tf_op jit(solution)/shard_map/dot_general | solution.py:9
  9.2 1.6 %fusion.8 = f32[64,512]{1,0:T(8,128)S(1)} fusion(f32[2,512,256]{2,1,0:T(8,128)} %param.5, f32[2,64,256]{2,1,0:T(8,128)S(1)} %broadcast_multiply_fusion), kind=kOutput, calls=%fused_computation.12 | convolution fusion | flops 100663296 | bytes 720896 | tf_op jit(solution)/shard_map/dot_general | solution.py:12
  10.8 0.0 copy-done
  10.9 0.6 fusion.1
  11.5 0.6 fusion
  12.1 0.7 pad_maximum_fusion
  12.8 0.0 copy-start.2
  12.8 0.0 all-reduce.2.cloned.1.call-update
  12.8 0.7 copy-done.2
  13.6 32.6 %all_gather.3 = f32[64,2,512]{2,0,1:T(8,128)S(1)} all-gather(f32[8,2,512]{2,0,1:T(8,128)S(1)} %copy.5), channel_id=1, replica_groups=mesh['grp'=2,'pts'=8,'rcv'=2] {'pts'}, dimensions={0}, use_global_device_ids=true | all-gather | bytes 294912 | tf_op jit(solution)/shard_map/all_gather | solution.py:43
  46.1 40.9 %all-reduce.2.cloned.1.call-done = f32[64,2,512]{2,0,1:T(8,128)} async-done(((f32[64,2,512]{2,0,1:T(8,128)}), f32[64,2,512]{2,0,1:T(8,128)}) %all-reduce.2.cloned.1.call-update) | async-done | bytes 262160 | tf_op jit(solution)/shard_map/psum | solution.py:44
  87.1 1.0 sub.10
  88.1 0.6 fusion.27
  88.7 3.1 %psum.22 = f32[]{:T(128)} all-reduce(f32[]{:T(128)} %fusion.27), channel_id=1, replica_groups=mesh['grp'=2,'pts'=8,'rcv'=2] {'rcv'}, use_global_device_ids=true, to_apply=%region_2.0 | all-reduce | flops 1 | bytes 8 | tf_op jit(solution)/shard_map/psum | solution.py:47
  92.5 0.4 fusion.13
  92.9 0.0 copy-start.1
  92.9 0.4 fusion.11
  93.3 0.5 copy-done.1
  93.8 0.4 fusion.4
  94.2 0.4 fusion.5
  94.6 2.5 %psum.23 = f32[256]{0:T(256)S(1)} all-reduce(f32[256]{0:T(256)S(1)} %fusion.5), channel_id=1, replica_groups=mesh['grp'=2,'pts'=8,'rcv'=2] {'rcv'}, use_global_device_ids=true, to_apply=%region_4.0 | all-reduce | flops 256 | bytes 2048 | tf_op jit(solution)/shard_map/psum | solution.py:51
  97.0 0.6 broadcast_multiply_fusion.1
  (3 shorter events, 0.1 us)
Async XLA Ops:
  6.5 4.3 %copy-start = (f32[2,512,256]{2,1,0:T(8,128)S(1)}, f32[2,512,256]{2,1,0:T(8,128)}, u32[]{:S(2)}) copy-start(f32[2,512,256]{2,1,0:T(8,128)} %param.5) | copy-start | bytes 3145732
  6.5 80.5 %all-reduce.2.cloned.1.call-start = ((), (), s32[]{:S(2)}) async-start(), calls=%async_computation | async-start | bytes 524288 | tf_op jit(solution)/shard_map/psum | solution.py:44
  12.8 0.8 copy-start.2
  92.9 0.9 copy-start.1
Sparse Core Ops, SparseCore 0:
  12.9 74.0 all-reduce.1
where the time goes:
time: 105 us; the launch traced here: 104 us
  waiting for transfers between devices  40.9 us (39%)
  blocking collectives  38.1 us (36%)
  between operations  14.1 us (13%)
  matrix products  6.05 us (6%)
  other arithmetic  3.97 us (4%)
  local copies, waits for them, and re-layouts  1.26 us (1%)
    psum x1, waiting for transfers between devices, local(): modelled = lax.psum(modelled_data(scaled, rcv_green), 'pts')  40.9 us
    all_gather x1, blocking collectives, local(): all_observed = lax.all_gather(observed, 'pts', axis=0, tiled=True)  32.6 us
    psum x1, blocking collectives, local(): total = lax.psum(energy_sum, 'rcv')  3.08 us
    psum x1, blocking collectives, local(): image = lax.psum(partial_image, 'rcv')  2.47 us
  transfers between devices with their start and end apart: 1, of which 1 were waited for; matrix products, arithmetic and copies ran while one was open for 0% of the time, Pallas kernels for 0%

commit v1 on v0

--- a/solution.py
+++ b/solution.py
@@ -2,6 +2,10 @@
 import jax.numpy as jnp
 from jax import lax
 from jax.sharding import PartitionSpec as P
+
+
+def scan_counts(packet, mesh_ax):
+    return lax.all_gather(packet, mesh_ax).sum(axis=0)
 
 
 def modelled_data(scaled, rcv_green):
@@ -41,7 +45,7 @@
     num_receivers = rcv_green.shape[1] * lax.axis_size("rcv")
     scaled = src_green * model[None, None, :]
     all_observed = lax.all_gather(observed, "pts", axis=0, tiled=True)
-    modelled = lax.psum(modelled_data(scaled, rcv_green), "pts")
+    modelled = scan_counts(modelled_data(scaled, rcv_green), "pts")
     resid = modelled - all_observed
     energy_sum = jnp.sum(resid[:, 0, :] ** 2 + resid[:, 1, :] ** 2)
     total = lax.psum(energy_sum, "rcv")

time: 105 us -> 84.4 us (0.80)
  waiting for transfers between devices: 40.9 us -> 19.4 us
  local copies, waits for them, and re-layouts: 1.26 us -> 0.02 us
    psum x1 -> x0, waiting for transfers between devices: 40.9 us -> none  [local(): modelled = lax.psum(modelled_data(scaled, rcv_green), 'pts')]
    all_gather x0 -> x1, waiting for transfers between devices: none -> 19.3 us  [scan_counts(): return lax.all_gather(packet, mesh_ax).sum(axis=0)]
    reduce_sum x0 -> x1, other arithmetic: none -> 1.82 us  [scan_counts(): return lax.all_gather(packet, mesh_ax).sum(axis=0)]
    unnamed x7, local copies, waits for them, and re-layouts: 1.26 us -> 0.02 us
where the time goes in v1:
time: 84.4 us; the launch traced here: 84.1 us
  blocking collectives  38.6 us (46%)
  waiting for transfers between devices  19.4 us (23%)
  between operations  14.1 us (17%)
  matrix products  7.09 us (8%)
  other arithmetic  4.87 us (6%)
    all_gather x1, blocking collectives, local(): all_observed = lax.all_gather(observed, 'pts', axis=0, tiled=True)  33.1 us
    all_gather x1, waiting for transfers between devices, scan_counts(): return lax.all_gather(packet, mesh_ax).sum(axis=0)  19.3 us
    psum x1, blocking collectives, local(): total = lax.psum(energy_sum, 'rcv')  3.08 us
    psum x1, blocking collectives, local(): image = lax.psum(partial_image, 'rcv')  2.47 us
    reduce_sum x1, other arithmetic, scan_counts(): return lax.all_gather(packet, mesh_ax).sum(axis=0)  1.82 us
  transfers between devices with their start and end apart: 1, of which 1 were waited for; matrix products, arithmetic and copies ran while one was open for 0% of the time, Pallas kernels for 0%

profile of v1, /device:TPU:0, one launch (start us, length us, event | category | flops | bytes accessed | tf_op | source)
XLA Modules:
  0.0 84.1 jit_solution(8579511648600364353)
XLA Ops:
  6.5 0.0 copy-start
  6.5 0.0 copy-start.2
  6.5 0.0 all-gather.3.cloned.1.call-start
  6.5 1.0 %broadcast_multiply_fusion = f32[2,64,256]{2,1,0:T(8,128)S(1)} fusion(f32[2,64,256]{2,1,0:T(8,128)} %param.4, f32[256]{0:T(256)} %param.6), kind=kLoop, calls=%fused_computation.40 | loop fusion | flops 32768 | bytes 263168 | tf_op jit(solution)/shard_map/mul | solution.py:46
  7.5 1.6 %fusion.16 = f32[64,512]{1,0:T(8,128)S(1)} fusion(f32[2,512,256]{2,1,0:T(8,128)} %param.5, f32[2,64,256]{2,1,0:T(8,128)S(1)} %broadcast_multiply_fusion), kind=kOutput, calls=%fused_computation.20 | convolution fusion | flops 100663296 | bytes 720896 | tf_op jit(solution)/shard_map/dot_general | solution.py:13
  9.2 1.6 %fusion.8 = f32[64,512]{1,0:T(8,128)S(1)} fusion(f32[2,512,256]{2,1,0:T(8,128)} %param.5, f32[2,64,256]{2,1,0:T(8,128)S(1)} %broadcast_multiply_fusion), kind=kOutput, calls=%fused_computation.12 | convolution fusion | flops 100663296 | bytes 720896 | tf_op jit(solution)/shard_map/dot_general | solution.py:16
  10.8 1.7 %fusion.1 = f32[64,1,512]{2,0,1:T(8,128)S(1)} fusion(f32[64,512]{1,0:T(8,128)S(1)} %fusion.16, f32[2,512,256]{2,1,0:T(8,128)} %param.5, f32[2,64,256]{2,1,0:T(8,128)S(1)} %broadcast_multiply_fusion), kind=kOutput, calls=%fused_computation.3 | convolution fusion | flops 100696064 | bytes 851968 | tf_op jit(solution)/shard_map/dot_general | solution.py:15
  12.5 0.0 copy-done
  12.5 0.6 fusion
  13.1 0.7 pad_maximum_fusion
  13.9 0.0 all-gather.3.cloned.1.call-update
  13.9 0.0 copy-done.2
  13.9 33.1 %all_gather.11 = f32[64,2,512]{2,0,1:T(8,128)S(1)} all-gather(f32[8,2,512]{2,0,1:T(8,128)S(1)} %copy.5), channel_id=1, replica_groups=mesh['grp'=2,'pts'=8,'rcv'=2] {'pts'}, dimensions={0}, use_global_device_ids=true | all-gather | bytes 294912 | tf_op jit(solution)/shard_map/all_gather | solution.py:47
  47.0 19.3 %all-gather.3.cloned.1.call-done = f32[512,2,512]{2,0,1:T(8,128)} async-done(((f32[64,2,512]{2,0,1:T(8,128)}), f32[512,2,512]{2,0,1:T(8,128)}) %all-gather.3.cloned.1.call-update) | async-done | bytes 2097168 | tf_op jit(solution)/shard_map/all_gather | solution.py:8
  66.3 1.8 %reduce_sum.27 = f32[64,2,512]{2,0,1:T(8,128)S(1)} reduce(f32[8,64,2,512]{3,1,0,2:T(8,128)} %bitcast.45, f32[]{:T(128)} %constant.1.clone.1), dimensions={0}, to_apply=%region_0.0 | reduce | flops 458752 | bytes 2359300 | tf_op jit(solution)/shard_map/reduce_sum | solution.py:8
  68.1 0.0 copy-start.1
  68.2 0.6 fusion.27
  68.8 3.1 %psum.14 = f32[]{:T(128)} all-reduce(f32[]{:T(128)} %fusion.27), channel_id=1, replica_groups=mesh['grp'=2,'pts'=8,'rcv'=2] {'rcv'}, use_global_device_ids=true, to_apply=%region_2.0 | all-reduce | flops 1 | bytes 8 | tf_op jit(solution)/shard_map/psum | solution.py:51
  72.6 0.4 fusion.13
  73.0 0.4 fusion.11
  73.4 0.0 copy-done.1
  73.4 0.4 fusion.4
  73.8 0.4 fusion.5
  74.2 2.5 %psum.15 = f32[256]{0:T(256)S(1)} all-reduce(f32[256]{0:T(256)S(1)} %fusion.5), channel_id=1, replica_groups=mesh['grp'=2,'pts'=8,'rcv'=2] {'rcv'}, use_global_device_ids=true, to_apply=%region_4.0 | all-reduce | flops 256 | bytes 2048 | tf_op jit(solution)/shard_map/psum | solution.py:55
  76.7 0.6 broadcast_multiply_fusion.1
  (4 shorter events, 0.1 us)
Async XLA Ops:
  6.5 6.0 %copy-start = (f32[2,512,256]{2,1,0:T(8,128)S(1)}, f32[2,512,256]{2,1,0:T(8,128)}, u32[]{:S(2)}) copy-start(f32[2,512,256]{2,1,0:T(8,128)} %param.5) | copy-start | bytes 3145732
  6.5 7.4 %copy-start.2 = (f32[8,2,512]{2,1,0:T(2,128)S(1)}, f32[8,2,512]{2,1,0:T(2,128)}, u32[]{:S(2)}) copy-start(f32[8,2,512]{2,1,0:T(2,128)} %param.7) | copy-start | bytes 98308
  6.5 59.8 %all-gather.3.cloned.1.call-start = ((), (), s32[]{:S(2)}) async-start(), calls=%async_computation | async-start | bytes 2359296 | tf_op jit(solution)/shard_map/all_gather | solution.py:8
  68.1 5.3 %copy-start.1 = (f32[2,64,256]{2,1,0:T(8,128)S(1)}, f32[2,64,256]{2,1,0:T(8,128)}, u32[]{:S(2)}) copy-start(f32[2,64,256]{2,1,0:T(8,128)} %param.4) | copy-start | bytes 393220
Sparse Core Ops, SparseCore 0:
  14.0 52.2 all-gather.2
